TPU v7x, 32 devices: a whole 2x2x4 slice. The times are simulated.
32 devices in a mesh: stream: 2 (over y), dp: 16 (over z, x, core).
Axes of the slice: x: 2, y: 2, z: 4, core: 2. Of those that a mesh axis runs over, the one named last changes fastest.
Arguments:
- hidden: bfloat16 [2, 64, 100, 1024], P('stream', 'dp'), may hold values from -6 to 6
- text_lengths: int32 [64], P('dp'), may hold values from 24 to 64
- region_counts: int32 [64], P('dp'), may hold values from 10 to 100
- co_qkv: bfloat16 [2, 3, 1024, 1024], P('stream'), may hold values from -0.1875 to 0.1875
- co_out: bfloat16 [2, 1024, 1024], P('stream'), may hold values from -1 to 1
- self_qkv: bfloat16 [2, 3, 1024, 1024], P('stream'), may hold values from -0.1875 to 0.1875
- self_out: bfloat16 [2, 1024, 1024], P('stream'), may hold values from -1 to 1
- mlp_up: bfloat16 [2, 2, 1024, 3072], P('stream'), may hold values from -0.1875 to 0.1875
- mlp_down: bfloat16 [2, 2, 3072, 1024], P('stream'), may hold values from -0.21875 to 0.21875
- proj_bias: bfloat16 [2, 2, 3, 1024], P('stream'), may hold values from -1.796875 to 1.796875
- mlp_bias_up: bfloat16 [2, 2, 3072], P('stream'), may hold values from -1.796875 to 1.796875
- mlp_bias_down: bfloat16 [2, 2, 1024], P('stream'), may hold values from -1.796875 to 1.796875
- norm_gain_table: bfloat16 [2, 4, 1024], P('stream'), may hold values from 0.099609375 to 1.8984375
- norm_bias: bfloat16 [2, 4, 1024], P('stream'), may hold values from -1.796875 to 1.796875
- cotangent: bfloat16 [2, 64, 100, 1024], P('stream', 'dp'), may hold values from -6 to 6
Outputs:
- result: bfloat16 [2, 64, 100, 1024], P('stream', 'dp')
- hidden_grad: bfloat16 [2, 64, 100, 1024], P('stream', 'dp')
- grad_co_qkv: float32 [2, 3, 1024, 1024], P('stream', None, 'dp')
- grad_co_out: float32 [2, 1024, 1024], P('stream', 'dp')
- grad_self_qkv: float32 [2, 3, 1024, 1024], P('stream', None, 'dp')
- grad_self_out: float32 [2, 1024, 1024], P('stream', 'dp')
- grad_mlp_up: float32 [2, 2, 1024, 3072], P('stream', None, 'dp')
- grad_mlp_down: float32 [2, 2, 3072, 1024], P('stream', None, 'dp')
- grad_proj_bias: float32 [2, 2, 3, 1024], P('stream', None, None, 'dp')
- grad_mlp_bias_up: float32 [2, 2, 3072], P('stream', None, 'dp')
- grad_mlp_bias_down: float32 [2, 2, 1024], P('stream', None, 'dp')
- grad_norm_gain: float32 [2, 4, 1024], P('stream', None, 'dp')
- grad_norm_bias: float32 [2, 4, 1024], P('stream', None, 'dp')
All inputs are finite; a program needn't handle non-finite values.
Results may differ from a plain program's by a relative error of at most 0.023.
Values may be sent and summed in bfloat16 or wider, within the bound.
A program may use at most 384 MiB of HBM per device.

v0:
```python
from functools import partial
from typing import NamedTuple
import math

import jax
import jax.numpy as jnp
from jax import lax
from jax.experimental import pallas as pl
from jax.experimental.pallas import tpu as pltpu
from jax.sharding import PartitionSpec as P

EPSILON = 1e-05
NEGATIVE = -1000000000.0
ROOT_HALF = 1.0 / math.sqrt(2.0)
GAUSS_NORM = 1.0 / math.sqrt(2.0 * math.pi)

MESH = pl.DeviceIdType.MESH
UNIT = 256
OUT_BLOCKS = 81
CORE_SLOTS = 4
Z_SLOTS = 6
SUM_LAG = 1
SUM_SLOTS = 4
VMEM_BYTES = 65200 * 1024

TEXT_UNITS = (
    (3, 3, 9, 1, 60, 0, 68, 4, 256),
    (1, 12, 5, 0, 44, 0, 44, 0, 192),
    (1, 3, 3, 0, 28, 0, 28, 0, 192),
    (3, 3, 2, 0, 16, 4, 16, 4, 192),
    (3, 3, 6, 1, 56, 0, 56, 4, 256),
    (1, 12, 4, 0, 32, 0, 32, 0, 192),
    (1, 3, 1, 0, 12, 0, 12, 0, 256),
    (3, 4, 0, 0, 0, 4, 0, 4, 192),
    (1, 1, 0, 0, 0, 0, 80, 0, 256),
)
IMAGE_UNITS = (
    (3, 4, 9, 1, 60, 0, 68, 4, 128),
    (1, 4, 5, 0, 44, 0, 44, 0, 256),
    (1, 4, 3, 0, 28, 0, 28, 0, 256),
    (3, 4, 2, 0, 16, 4, 16, 4, 256),
    (3, 4, 6, 1, 56, 0, 56, 4, 128),
    (1, 4, 4, 0, 32, 0, 32, 0, 256),
    (1, 4, 1, 0, 12, 0, 12, 0, 256),
    (3, 4, 0, 0, 0, 4, 0, 4, 256),
    (1, 1, 0, 0, 0, 0, 80, 0, 256),
)


def side_lag(line):
    return 6 if line <= 8 else 4


def line_lag(line):
    return 3 if line <= 8 else 1


def slots_held(line):
    return side_lag(line) + (line - 1) * line_lag(line) + 1 + SUM_LAG


def unit_count(table):
    return sum(entry[0] * entry[1] for entry in table)


def decode_one(table, unit):
    start = 0
    result = None
    for groups, blocks, a0, a1, g0, g1, o0, o1, kept in table:
        local = unit - start
        group = local // blocks
        block = local % blocks
        fields = (a0 + a1 * group, g0 + g1 * group + block, o0 + o1 * group + block, jnp.int32(kept))
        if result is None:
            result = fields
        else:
            result = tuple(jnp.where(unit >= start, new, old) for new, old in zip(fields, result))
        start += groups * blocks
    return result


def kept_one(table, unit):
    start = 0
    result = jnp.int32(table[0][-1])
    before = table[0][-1]
    for groups, blocks, *_, kept in table:
        if kept != before:
            result = jnp.where(unit >= start, kept, result)
            before = kept
        start += groups * blocks
    return result


def rows_kept(is_text, unit):
    return jnp.where(is_text, kept_one(TEXT_UNITS, unit), kept_one(IMAGE_UNITS, unit))


def decode(is_text, unit):
    text = decode_one(TEXT_UNITS, unit)
    image = decode_one(IMAGE_UNITS, unit)
    return tuple(jnp.where(is_text, one, other) for one, other in zip(text, image))


SENT = 104


class Stream(NamedTuple):
    asks: bool
    width: int
    inner: int
    split: int
    head: int
    own_keys: int
    order: tuple


SHORT = 64
TEXT = Stream(True, 768, 3072, 2, 64, SHORT, (0, 1, 2))
IMAGE = Stream(False, 1024, 1024, 1, 128, 112, (1, 2, 0))
TEXT_PACE = (36, 55, 4)
IMAGE_PACE = (42, 54, 4)
RING = 3
LANES = 128
TAIL = (
    0.28208317669832234,
    0.2824362970929616,
    0.24263030272423752,
    0.20467309203585946,
    -0.03157028123874516,
    0.28558060664263174,
    -0.4940359058844012,
    0.2879944144937219,
    -0.0597917499304742,
)


def gelu_parts(value):
    root = jnp.abs(value) * ROOT_HALF
    near = 1.0 / (1.0 + 0.5 * root)
    bell = jnp.exp(-(root * root))
    series = TAIL[-1] * near
    for factor in TAIL[-2::-1]:
        series = (series + factor) * near
    tail = 0.5 * bell * series
    below = jnp.where(value >= 0.0, 1.0 - tail, tail)
    return value * below, below + value * bell * GAUSS_NORM


def layer_kernel(
    line,
    pairs,
    slots,
    tall,
    text_lengths,
    region_counts,
    hidden,
    cotangent,
    co_qkv_whole,
    co_out_whole,
    self_qkv_whole,
    self_out_whole,
    mlp_up_whole,
    mlp_down_whole,
    proj_bias,
    bias_up,
    bias_down,
    gain,
    shift,
    result,
    grad,
    sums_out,
    at_ref,
    g_ref,
    vectors,
    hidden_vectors,
    staged,
    ring,
    far,
    far_query,
    state,
    total,
    low,
    active,
    normal,
    spread,
    self_probs,
    co_probs,
    params,
    up_params,
    ring_sems,
    send_sems,
    recv_sems,
    back_send_sems,
    back_recv_sems,
    landing_free,
    staged_sems,
    core_out,
    core_in,
    partial_own,
    x_out,
    x_in,
    own,
    down_out,
    down_in,
    up_out,
    up_in,
    core_sems,
    x_sems,
    down_sems,
    up_sems,
    down_free,
    up_free,
    sum_sems,
    blank_sems,
):
    stream = lax.axis_index("stream")
    place = lax.axis_index("dp")
    partner = (1 - stream, place)
    height = pairs * tall
    piece = 256 // line
    per_block = 256 // piece

    core = lax.rem(place, 2)
    side = lax.rem(place // 2, 2)
    spot = place // 4
    is_text = stream == 0
    unit_total = jnp.where(is_text, unit_count(TEXT_UNITS), unit_count(IMAGE_UNITS))
    core_device = (stream, place + 1 - 2 * core)
    side_device = (stream, place + 2 - 4 * side)
    lower_device = (stream, place - 4)
    upper_device = (stream, place + 4)
    own_slots = slots_held(line)
    last = line - 1
    co_qkv, co_out, self_qkv, self_out, mlp_up, mlp_down = (
        ref.at[0]
        for ref in (
            co_qkv_whole,
            co_out_whole,
            self_qkv_whole,
            self_out_whole,
            mlp_up_whole,
            mlp_down_whole,
        )
    )
    hidden_ref, cotangent_ref = staged.at[0], staged.at[1]
    result_ref, grad_ref = staged.at[0], staged.at[1]

    def stage(index):
        source = (hidden, cotangent)[index]
        return pltpu.make_async_copy(source.at[0], staged.at[index], staged_sems.at[index])

    def unstage(index):
        target = (result, grad)[index]
        return pltpu.make_async_copy(staged.at[index], target.at[0], staged_sems.at[index])

    stage(0).start()
    stage(1).start()
    far[...] = jnp.zeros_like(far)
    far_query[...] = jnp.zeros_like(far_query)

    barrier = pltpu.get_barrier_semaphore()
    for device in (partner, core_device, side_device):
        pl.semaphore_signal(barrier, inc=1, device_id=device, device_id_type=MESH)

    @pl.when(spot > 0)
    def _():
        pl.semaphore_signal(barrier, inc=1, device_id=lower_device, device_id_type=MESH)

    @pl.when(spot < last)
    def _():
        pl.semaphore_signal(barrier, inc=1, device_id=upper_device, device_id_type=MESH)

    pl.semaphore_wait(
        barrier, 3 + (spot > 0).astype(jnp.int32) + (spot < last).astype(jnp.int32)
    )
    for half in range(2):
        params[3 * half : 3 * half + 3] = proj_bias[0, half].astype(jnp.float32)
    params[6:8] = bias_down[0].astype(jnp.float32)
    params[8:12] = gain[0].astype(jnp.float32)
    params[12:16] = shift[0].astype(jnp.float32)
    up_params[0:2] = bias_up[0].astype(jnp.float32)
    vectors[...] = jnp.zeros_like(vectors)
    hidden_vectors[...] = jnp.zeros_like(hidden_vectors)

    state[0:piece] = jnp.zeros((piece, 1024), jnp.float32)

    def blank(index):
        width = min(1024, OUT_BLOCKS * UNIT - index * 1024)
        return pltpu.make_async_copy(
            state.at[pl.ds(0, piece), pl.ds(0, width)],
            sums_out.at[:, pl.ds(index * 1024, width)],
            blank_sems.at[index],
        )

    blanks = [blank(index) for index in range(-(-OUT_BLOCKS * UNIT // 1024))]
    for copy in blanks:
        copy.start()

    def block(index):
        return pl.ds(pl.multiple_of(index * UNIT, UNIT), UNIT)

    def pair_rows(pair, count=tall):
        return pl.ds(pl.multiple_of(pair * tall, tall), count)

    def exchange(source, source_at, target, target_at, sends, receives, which, pair):
        return pltpu.make_async_remote_copy(
            src_ref=source.at[source_at],
            dst_ref=target.at[target_at],
            send_sem=sends.at[which, pair],
            recv_sem=receives.at[which, pair],
            device_id=partner,
            device_id_type=MESH,
        )

    def short_rows(which, pair):
        return pl.ds(
            pl.multiple_of((which * pairs + pair) * SHORT, SHORT), SHORT
        )

    def ask(pair):
        at = pair_rows(pair, SENT)
        return exchange(g_ref.at[0], at, far_query, at, send_sems, recv_sems, 0, pair)

    def hand(which, pair):
        return exchange(
            g_ref.at[1 + which],
            pair_rows(pair, SHORT),
            far,
            short_rows(which, pair),
            send_sems,
            recv_sems,
            1 + which,
            pair,
        )

    def answer(pair):
        at = pair_rows(pair, SENT)
        return exchange(active, at, far, at, send_sems, recv_sems, 0, pair)

    def ask_back(pair):
        at = pair_rows(pair, SENT)
        return exchange(low, at, active, at, back_send_sems, back_recv_sems, 0, pair)

    def hand_back(which, pair):
        return exchange(
            far,
            short_rows(which, pair),
            g_ref.at[1 + which],
            pair_rows(pair, SHORT),
            back_send_sems,
            back_recv_sems,
            1 + which,
            pair,
        )

    def answer_back(pair):
        at = pair_rows(pair, SENT)
        return exchange(far_query, at, g_ref.at[0], at, back_send_sems, back_recv_sems, 0, pair)

    def for_rows(kept, body):
        for rows in (128, 192, 256):

            @pl.when(kept == rows)
            def _():
                body(rows)

    def core_copy(unit, rows):
        slot = lax.rem(unit, CORE_SLOTS)
        return pltpu.make_async_remote_copy(
            src_ref=core_out.at[slot, :, pl.ds(0, rows)],
            dst_ref=core_in.at[slot, :, pl.ds(0, rows)],
            send_sem=core_sems.at[0, slot],
            recv_sem=core_sems.at[1, slot],
            device_id=core_device,
            device_id_type=MESH,
        )

    def side_copy(unit, rows):
        slot = lax.rem(unit, 2 * side_lag(line))
        return pltpu.make_async_remote_copy(
            src_ref=x_out.at[slot, pl.ds(0, rows)],
            dst_ref=x_in.at[slot, pl.ds(0, rows)],
            send_sem=x_sems.at[0, slot],
            recv_sem=x_sems.at[1, slot],
            device_id=side_device,
            device_id_type=MESH,
        )

    def line_copy(source, target, sems, device, slot, index):
        at = pl.ds(pl.multiple_of(index * piece, piece), piece)
        return pltpu.make_async_remote_copy(
            src_ref=source.at[slot, at],
            dst_ref=target.at[slot, at],
            send_sem=sems.at[0, slot, index],
            recv_sem=sems.at[1, slot, index],
            device_id=device,
            device_id_type=MESH,
        )

    def columns(block):
        return pl.ds(pl.multiple_of(block * UNIT, UNIT), UNIT)

    def multiply(unit):
        a_block, g_block, out_block, kept = decode(is_text, unit)
        slot = lax.rem(unit, CORE_SLOTS)
        keep = lax.rem(unit, 2)
        is_vector = unit == unit_total - 1

        @pl.when(jnp.logical_not(is_vector))
        def _():
            gradient = g_ref[g_block // 4, :, columns(lax.rem(g_block, 4))]

            def body(rows):
                def product(which):
                    operand = at_ref[a_block, which, :, pl.ds(0, rows)]
                    return jnp.dot(
                        operand.reshape(2 * rows, operand.shape[-1]),
                        gradient,
                        preferred_element_type=jnp.float32,
                    ).reshape(2, rows, UNIT)

                core_out[slot, :, pl.ds(0, rows)] = product(1 - core).astype(jnp.bfloat16)
                core_copy(unit, rows).start()
                partial_own[keep, :, pl.ds(0, rows)] = product(core)

            for_rows(kept, body)

        @pl.when(is_vector)
        def _():
            place_vectors(slot, keep)
            core_copy(unit, 256).start()

    def add_core(unit):
        kept = rows_kept(is_text, unit)
        slot = lax.rem(unit, CORE_SLOTS)
        keep = lax.rem(unit, 2)
        far = lax.rem(unit, 2 * side_lag(line))
        store = lax.rem(unit, own_slots)

        def body(rows):
            core_copy(unit, rows).wait()
            at = pl.ds(0, rows)
            x_out[far, at] = (
                partial_own[keep, 1 - side, at] + core_in[slot, 1 - side, at].astype(jnp.float32)
            ).astype(jnp.bfloat16)
            side_copy(unit, rows).start()
            own[store, at] = partial_own[keep, side, at] + core_in[slot, side, at].astype(
                jnp.float32
            )

        for_rows(kept, body)

    def add_side(unit):
        kept = rows_kept(is_text, unit)
        far = lax.rem(unit, 2 * side_lag(line))
        store = lax.rem(unit, own_slots)

        def body(rows):
            side_copy(unit, rows).wait()
            at = pl.ds(0, rows)
            own[store, at] += x_in[far, at].astype(jnp.float32)

        for_rows(kept, body)

    def sum_copy(unit, out_block):
        at = pl.ds(pl.multiple_of(spot * piece, piece), piece)
        return pltpu.make_async_copy(
            own.at[lax.rem(unit, own_slots), at],
            sums_out.at[:, columns(out_block)],
            sum_sems.at[lax.rem(unit, SUM_SLOTS)],
        )

    def has_sum(unit):
        return (spot + 1) * piece <= rows_kept(is_text, unit)

    def line_step(unit, source, target, sems, free, sender, reader, low, high, gives, takes):
        slot = lax.rem(unit + Z_SLOTS, Z_SLOTS)

        @pl.when(jnp.logical_and(unit >= Z_SLOTS, gives))
        def _():
            count = rows_kept(is_text, unit - Z_SLOTS) // piece
            pl.semaphore_wait(free, 1)

            def settle(index, carry):
                line_copy(source, target, sems, reader, slot, index).wait_send()
                return carry

            lax.fori_loop(low(count), high(count), settle, 0)

        @pl.when(unit < unit_total)
        def _():
            count = rows_kept(is_text, unit) // piece
            store = lax.rem(unit, own_slots)

            def at(index):
                return pl.ds(pl.multiple_of(index * piece, piece), piece)

            @pl.when(gives)
            def _():
                def forward(index, carry):
                    @pl.when(takes)
                    def _():
                        line_copy(source, target, sems, reader, slot, index).wait_recv()
                        source[slot, at(index)] = (
                            own[store, at(index)] + target[slot, at(index)].astype(jnp.float32)
                        ).astype(jnp.bfloat16)

                    @pl.when(jnp.logical_not(takes))
                    def _():
                        source[slot, at(index)] = own[store, at(index)].astype(jnp.bfloat16)

                    line_copy(source, target, sems, reader, slot, index).start()
                    return carry

                lax.fori_loop(low(count), high(count), forward, 0)

            @pl.when(takes)
            def _():
                @pl.when(spot < count)
                def _():
                    line_copy(source, target, sems, reader, slot, spot).wait_recv()
                    own[store, at(spot)] += target[slot, at(spot)].astype(jnp.float32)

                pl.semaphore_signal(free, inc=1, device_id=sender, device_id_type=MESH)

    def tick(step):
        @pl.when(step < unit_total)
        def _():
            multiply(step)

        @pl.when(jnp.logical_and(step >= 1, step < unit_total + 1))
        def _():
            add_core(step - 1)

        @pl.when(jnp.logical_and(step >= side_lag(line), step < unit_total + side_lag(line)))
        def _():
            add_side(step - side_lag(line))

        falling = step - side_lag(line) - (last - spot) * line_lag(line)

        @pl.when(jnp.logical_and(falling >= 0, falling < unit_total + Z_SLOTS))
        def _():
            line_step(
                falling,
                down_out,
                down_in,
                down_sems,
                down_free,
                upper_device,
                lower_device,
                lambda count: 0,
                lambda count: jnp.minimum(spot, count),
                spot > 0,
                spot < last,
            )

        rising = step - side_lag(line) - spot * line_lag(line)

        @pl.when(jnp.logical_and(rising >= 0, rising < unit_total + Z_SLOTS))
        def _():
            line_step(
                rising,
                up_out,
                up_in,
                up_sems,
                up_free,
                lower_device,
                upper_device,
                lambda count: jnp.minimum(spot + 1, count),
                lambda count: count,
                spot < last,
                spot > 0,
            )

        final = step - side_lag(line) - last * line_lag(line)

        @pl.when(jnp.logical_and(final >= 0, final < unit_total))
        def _():
            pl.when(has_sum(final))(lambda: sum_copy(final, decode(is_text, final)[2]).start())

        settled = final - SUM_LAG

        @pl.when(jnp.logical_and(settled >= 0, settled < unit_total))
        def _():
            pl.when(has_sum(settled))(lambda: sum_copy(settled, 0).wait())

    def place_vectors(slot, keep):
        turned = jnp.concatenate(
            [vectors[...], jnp.zeros((LANES - 32, 1024), jnp.float32)], axis=0
        ).T
        tall_sums = hidden_vectors[...].T
        lane = lax.broadcasted_iota(jnp.int32, (piece, LANES), 1)
        for owner in range(4 * line):
            value = turned[owner * piece : (owner + 1) * piece]
            for group in range(3):
                number = owner * 3 + group
                part = tall_sums[number * piece : (number + 1) * piece]
                for which in range(2):
                    value = jnp.where(
                        lane == 6 + 3 * which + group, part[:, which : which + 1], value
                    )
            total[
                owner // 8 * piece : (owner // 8 + 1) * piece,
                owner % 8 * LANES : (owner % 8 + 1) * LANES,
            ] = value
        core_out[slot] = jnp.zeros((2, 256, UNIT), jnp.bfloat16)
        partial_own[keep] = jnp.zeros((2, 256, UNIT), jnp.float32)

        def step(owner, carry):
            value = total[
                pl.ds(pl.multiple_of(owner // 8 * piece, piece), piece),
                pl.ds(pl.multiple_of(lax.rem(owner, 8) * LANES, LANES), LANES),
            ]
            at = pl.ds(pl.multiple_of((owner // 4) * piece, piece), piece)
            half = lax.rem(owner // 2, 2)

            @pl.when(lax.rem(owner, 2) == core)
            def _():
                partial_own[keep, half, at, 0:LANES] = value

            @pl.when(lax.rem(owner, 2) != core)
            def _():
                core_out[slot, half, at, 0:LANES] = value.astype(jnp.bfloat16)

            return carry

        lax.fori_loop(0, 4 * line, step, 0)

    def run(cfg, own_lengths, far_lengths):
        width, inner = cfg.width, cfg.inner
        chunks = inner // 1024
        groups = width // LANES

        plan = [co_qkv.at[index, pl.ds(0, width)] for index in cfg.order]
        plan.append(co_out.at[:, pl.ds(0, width)])

        def mlp_plan(index, chunk):
            at = pl.ds(chunk * 1024, 1024)
            return mlp_up.at[index, pl.ds(0, width), at], mlp_down.at[index, at, pl.ds(0, width)]

        def square(index):
            return self_qkv.at[index, pl.ds(0, width), pl.ds(0, width)]

        for chunk in range(chunks):
            plan.extend(mlp_plan(0, chunk))
        plan.extend(square(index) for index in range(3))
        plan.append(self_out.at[pl.ds(0, width), pl.ds(0, width)])
        for chunk in range(chunks):
            plan.extend(mlp_plan(1, chunk))
        for chunk in range(chunks):
            plan.extend(mlp_plan(1, chunk)[::-1])
        plan.append(self_out.at[pl.ds(0, width), pl.ds(0, width)])
        plan.extend(square(index) for index in range(3))
        for chunk in range(chunks):
            plan.extend(mlp_plan(0, chunk)[::-1])
        plan.append(co_out.at[:, pl.ds(0, width)])
        plan.extend(co_qkv.at[index, pl.ds(0, width)] for index in range(3))

        def fetch(index):
            rows, columns = plan[index].shape
            return pltpu.make_async_copy(
                plan[index],
                ring.at[index % RING, pl.ds(0, rows), pl.ds(0, columns)],
                ring_sems.at[index % RING],
            )

        used = [0]
        def with_weight(body):
            index = used[0]
            used[0] += 1
            fetch(index).wait()
            rows, columns = plan[index].shape
            body(ring.at[index % RING], rows, columns)
            if index + RING < len(plan):
                fetch(index + RING).start()

        def forward_product(source, consume):
            def body(weight, rows, columns):
                def step(index, carry):
                    consume(
                        index,
                        jnp.dot(
                            source[:, 0:rows],
                            weight[0:rows, block(index)],
                            preferred_element_type=jnp.float32,
                        ),
                    )
                    return carry

                lax.fori_loop(0, columns // UNIT, step, 0)

            with_weight(body)

        segments = []

        def backward_items(source, consume):
            index = used[0]
            used[0] += 1
            rows, columns = plan[index].shape
            weight = ring.at[index % RING]
            count = rows // UNIT

            def item(number):
                @pl.when(number == 0)
                def _():
                    fetch(index).wait()

                consume(
                    number,
                    lax.dot_general(
                        source[:, 0:columns],
                        weight[block(number), 0:columns],
                        (((1,), (1,)), ((), ())),
                        preferred_element_type=jnp.float32,
                    ),
                )
                if index + RING < len(plan):

                    @pl.when(number == count - 1)
                    def _():
                        fetch(index + RING).start()

            segments.append((count, item))

        def add_total(first):
            def consume(index, value):
                if first:
                    total[:, block(index)] = value
                else:
                    total[:, block(index)] += value

            return consume

        def put_rows(at_block, index, value):
            turned = value.T
            for part in range(per_block):
                at_ref[
                    at_block,
                    part % 2,
                    (part // 2) % 2,
                    pl.ds(pl.multiple_of((index * (per_block // 4) + part // 4) * piece, piece), piece),
                ] = turned[part * piece : (part + 1) * piece]

        def put_hidden_rows(at_block, index, value):
            turned = value.T
            for part in range(per_block):
                number = index * per_block + part
                owner = number // 3
                at_ref[
                    at_block + lax.rem(number, 3),
                    lax.rem(owner, 2),
                    lax.rem(owner // 2, 2),
                    pl.ds(pl.multiple_of((owner // 4) * piece, piece), piece),
                ] = turned[part * piece : (part + 1) * piece]

        def put_low(at_block, columns, source=low):
            def step(index, carry):
                put_rows(at_block, index, source[:, block(index)])
                return carry

            lax.fori_loop(0, columns // UNIT, step, 0)

        def for_pairs(body):
            def step(pair, carry):
                body(pair)
                return carry

            lax.fori_loop(0, pairs, step, 0)

        def mean(value):
            return jnp.sum(value, axis=-1, keepdims=True) * (1.0 / width)

        def normalize(value):
            centered = value - mean(value)
            inverse = lax.rsqrt(mean(centered * centered) + EPSILON)
            return centered * inverse, inverse

        def norm_forward(index, bias_row, at_block):
            def body(pair):
                at = pair_rows(pair)
                rows, inverse = normalize(
                    state[at, 0:width] + total[at, 0:width] + params[bias_row : bias_row + 1, 0:width]
                )
                result = (
                    rows * params[8 + index : 9 + index, 0:width]
                    + params[12 + index : 13 + index, 0:width]
                )
                state[at, 0:width] = result
                low[at, 0:width] = result.astype(jnp.bfloat16)
                normal[index, at, 0:width] = rows.astype(jnp.bfloat16)
                spread[at, index : index + 1] = inverse

            for_pairs(body)
            put_low(at_block, width)

        def add_row(ref, row, value):
            ref[row : row + 1, 0 : value.shape[-1]] += jnp.sum(value, axis=0, keepdims=True)

        def norm_gradient(index, at, gradient, rows, inverse, g_block, bias_row):
            scaled = gradient * params[8 + index : 9 + index, 0:width]
            result = inverse * (scaled - mean(scaled) - rows * mean(scaled * rows))
            state[at, 0:width] = result
            rounded = result.astype(jnp.bfloat16)
            g_ref[g_block, at, 0:width] = rounded
            add_row(vectors, 14 + index, gradient * rows)
            add_row(vectors, 18 + index, gradient)
            add_row(vectors, bias_row if bias_row < 6 else bias_row + 6, rounded.astype(jnp.float32))

        def norm_backward(index, g_block, bias_row):
            def body(pair):
                at = pair_rows(pair)
                norm_gradient(
                    index,
                    at,
                    state[at, 0:width] + total[at, 0:width],
                    normal[index, at, 0:width].astype(jnp.float32),
                    spread[at, index : index + 1],
                    g_block,
                    bias_row,
                )

            segments.append((pairs, body))

        def mlp_forward(index):
            for chunk in range(chunks):

                def activate(number, value):
                    act, slope = gelu_parts(
                        value
                        + up_params[
                            index : index + 1,
                            pl.ds(pl.multiple_of(chunk * 1024 + number * UNIT, UNIT), UNIT),
                        ]
                    )
                    act = act.astype(jnp.bfloat16)
                    active[:, block(number)] = act
                    g_ref[8 + 3 * index + chunk, :, block(number)] = slope.astype(jnp.bfloat16)
                    put_hidden_rows(6 + 3 * index, chunk * 4 + number, act)

                forward_product(low, activate)
                forward_product(active, add_total(chunk == 0))

        def mlp_backward(index):
            for chunk in range(chunks):
                g_block = 8 + 3 * index + chunk

                def through(number, value, g_block=g_block, chunk=chunk):
                    slope = g_ref[g_block, :, block(number)].astype(jnp.float32)
                    rounded = (value * slope).astype(jnp.bfloat16)
                    g_ref[g_block, :, block(number)] = rounded
                    hidden_vectors[
                        index : index + 1,
                        pl.ds(pl.multiple_of(chunk * 1024 + number * UNIT, UNIT), UNIT),
                    ] = jnp.sum(rounded.astype(jnp.float32), axis=0, keepdims=True)

                backward_items(g_ref.at[14 + index], through)
                backward_items(g_ref.at[g_block], add_total(chunk == 0))

        def biased(target, bias_row):
            def consume(index, value):
                if bias_row is not None:
                    value = value + params[bias_row : bias_row + 1, block(index)]
                target[:, block(index)] = value.astype(jnp.bfloat16)

            return consume

        def column_sums(g_block, row, columns):
            def item(index):
                vectors[row : row + 1, block(index)] = jnp.sum(
                    g_ref[g_block, :, block(index)].astype(jnp.float32), axis=0, keepdims=True
                )

            segments.append((columns // UNIT, item))

        def stacked(value, split):
            if split == 1:
                return value
            lane = lax.broadcasted_iota(jnp.int32, value.shape, 1)
            zero = jnp.zeros_like(value)
            return jnp.concatenate(
                [jnp.where(lane < 64, value, zero), jnp.where(lane < 64, zero, value)], axis=0
            )

        def unstacked(value, split):
            if split == 1:
                return value
            half = value.shape[0] // 2
            lane = lax.broadcasted_iota(jnp.int32, (half, LANES), 1)
            return jnp.where(lane < 64, value[:half], value[half:])

        def over_keys(reduce, value, split):
            if split == 1:
                return reduce(value, axis=0, keepdims=True)
            half = value.shape[0] // 2
            return jnp.concatenate(
                [
                    jnp.broadcast_to(
                        reduce(part, axis=0, keepdims=True), part.shape
                    )
                    for part in (value[:half], value[half:])
                ],
                axis=0,
            )

        last_last = (((1,), (1,)), ((), ()))
        first_first = (((0,), (0,)), ((), ()))

        def attend_forward(query, keys, values, key_rows, probs, target, lengths, split, head, group_count):
            scale = 1.0 / math.sqrt(head)

            def body(pair):
                length = lengths[pair]
                for group in range(group_count):
                    at = pl.ds(group * LANES, LANES)
                    key = stacked(keys[key_rows(pair), at], split)
                    value = stacked(values[key_rows(pair), at], split)
                    count = key.shape[0] // split
                    scores = (
                        lax.dot_general(
                            key,
                            query[pair_rows(pair), at],
                            last_last,
                            preferred_element_type=jnp.float32,
                        )
                        * scale
                    )
                    number = lax.broadcasted_iota(jnp.int32, scores.shape, 0)
                    if split == 2:
                        number = jnp.where(number < count, number, number - count)
                    scores = jnp.where(number < length, scores, NEGATIVE)
                    raised = jnp.exp(scores - over_keys(jnp.max, scores, split))
                    shares = (raised * (1.0 / over_keys(jnp.sum, raised, split))).astype(
                        jnp.bfloat16
                    )
                    probs[pair, group, 0 : count * split] = shares
                    target[pair_rows(pair), at] = lax.dot_general(
                        shares,
                        value,
                        first_first,
                        preferred_element_type=jnp.float32,
                    ).astype(jnp.bfloat16)

            return body

        def attend_backward(query, keys, values, key_rows, probs, source, split, head, group_count):
            scale = 1.0 / math.sqrt(head)

            def body(pair):
                for group in range(group_count):
                    at = pl.ds(group * LANES, LANES)
                    key = stacked(keys[key_rows(pair), at], split)
                    value = stacked(values[key_rows(pair), at], split)
                    count = key.shape[0] // split
                    asked = query[pair_rows(pair), at]
                    gradient = source[pair_rows(pair), at]
                    rounded_shares = probs[pair, group, 0 : count * split]
                    shares = rounded_shares.astype(jnp.float32)
                    grad_shares = lax.dot_general(
                        value, gradient, last_last, preferred_element_type=jnp.float32
                    )
                    grad_scores = (
                        shares
                        * (grad_shares - over_keys(jnp.sum, grad_shares * shares, split))
                        * scale
                    ).astype(jnp.bfloat16)
                    grad_value = unstacked(
                        jnp.dot(
                            rounded_shares,
                            gradient,
                            preferred_element_type=jnp.float32,
                        ),
                        split,
                    )
                    grad_key = unstacked(
                        jnp.dot(grad_scores, asked, preferred_element_type=jnp.float32), split
                    )
                    grad_query = lax.dot_general(
                        grad_scores, key, first_first, preferred_element_type=jnp.float32
                    )
                    query[pair_rows(pair), at] = grad_query.astype(jnp.bfloat16)
                    keys[key_rows(pair), at] = grad_key.astype(jnp.bfloat16)
                    values[key_rows(pair), at] = grad_value.astype(jnp.bfloat16)

            return body

        def clear_tail(ref, pair, count):
            if count < tall:
                at = pl.ds(pl.multiple_of(pair * tall + count, 16), tall - count)
                ref[at, :] = jnp.zeros((tall - count, ref.shape[-1]), ref.dtype)

        own_refs = (g_ref.at[1], g_ref.at[2])
        def clear_rest(ref, pair):
            ref[pair * tall + SENT : (pair + 1) * tall] = jnp.zeros((tall - SENT, 1024), ref.dtype)

        self_refs = (g_ref.at[4], g_ref.at[5], g_ref.at[6])
        short_refs = (far.at[pl.ds(0, pairs * SHORT)], far.at[pl.ds(pairs * SHORT, pairs * SHORT)])

        def own_rows(pair):
            return pair_rows(pair, cfg.own_keys)

        def far_rows(pair):
            return pl.ds(pl.multiple_of(pair * SHORT, SHORT), SHORT)

        near_attention = (g_ref.at[0], *short_refs, far_rows, co_probs.at[:, pl.ds(8, 8)])
        far_attention = (far_query, *own_refs, own_rows, co_probs.at[:, pl.ds(0, 8)])
        self_attention = (*self_refs, own_rows, self_probs)

        def forward():
            for index in range(RING):
                fetch(index).start()
            if inner < 3072:
                for which in range(6, 12):
                    at_ref[which, :, :, 0:128] = jnp.zeros((2, 2, 128, height), jnp.bfloat16)
            low[...] = jnp.zeros_like(low)
            stage(0).wait()
            for pair in range(pairs):
                low[pair * tall : pair * tall + slots, 0:width] = hidden_ref[pair, :, 0:width]
            for index in cfg.order:
                forward_product(low, biased(g_ref.at[index], (0, None, 1)[index]))
                if cfg.asks and index == 0:
                    for pair in range(pairs):
                        ask(pair).start()
            put_low(0, width)
            for copy in blanks:
                copy.wait()
            state[:, 0:width] = low[:, 0:width].astype(jnp.float32)
            if cfg.asks:
                for pair in range(pairs):
                    ask(pair).wait_send()
                    clear_rest(g_ref.at[0], pair)
                for which in range(2):
                    for pair in range(pairs):
                        hand(which, pair).start()
                for pair in range(pairs):
                    answer(pair).wait_recv()
                context = far.at[pl.ds(0, height)]
                put_low(1, 1024, context)
                forward_product(context, add_total(True))
                norm_forward(0, 2, 4)
            else:

                def reply(pair):
                    ask(pair).wait_recv()
                    attend_forward(*far_attention, active, own_lengths, 1, 128, 8)(pair)
                    answer(pair).start()

                for_pairs(reply)

                def attend(pair):
                    for which in range(2):
                        hand(which, pair).wait_recv()
                    attend_forward(*near_attention, low, far_lengths, 1, 128, 8)(pair)

                for_pairs(attend)
                for pair in range(pairs):
                    answer(pair).wait_send()
                put_low(1, 1024)
                forward_product(low, add_total(True))
                norm_forward(0, 2, 4)
            mlp_forward(0)
            norm_forward(1, 6, 2)
            if cfg.asks:
                for pair in range(pairs):
                    for which in range(2):
                        hand(which, pair).wait_send()
                        clear_tail(own_refs[which], pair, SHORT)
                pl.semaphore_signal(landing_free, inc=1, device_id=partner, device_id_type=MESH)
            for index, bias_row in ((0, 3), (1, None), (2, 4)):
                forward_product(low, biased(self_refs[index], bias_row))
            for_pairs(
                attend_forward(*self_attention, low, own_lengths, cfg.split, cfg.head, groups)
            )
            put_low(3, width)
            forward_product(low, add_total(True))
            norm_forward(2, 5, 5)
            mlp_forward(1)
            if not cfg.asks:
                for pair in range(pairs):
                    clear_rest(active, pair)
                pl.semaphore_signal(landing_free, inc=1, device_id=partner, device_id_type=MESH)

            if width < 1024:
                result_ref[...] = jnp.zeros_like(result_ref)
            stage(1).wait()

            def last_norm(pair):
                at = pair_rows(pair)
                rows, inverse = normalize(
                    state[at, 0:width] + total[at, 0:width] + params[7:8, 0:width]
                )
                result = rows * params[11:12, 0:width] + params[15:16, 0:width]
                result_ref[pair, :, 0:width] = result[0:slots].astype(jnp.bfloat16)
                total[at, 0:width] = jnp.zeros((tall, width), jnp.float32)
                total[pl.ds(pl.multiple_of(pair * tall, tall), slots), 0:width] = cotangent_ref[
                    pair, :, 0:width
                ].astype(jnp.float32)
                norm_gradient(3, at, total[at, 0:width], rows, inverse, 15, 7)

            for_pairs(last_norm)
            unstage(0).start()


        def self_attention_item(pair):
            attend_backward(*self_attention, low, cfg.split, cfg.head, groups)(pair)
            for ref in self_refs[1:]:
                clear_tail(ref, pair, cfg.own_keys)

        def partner_ready(pair):
            @pl.when(pair == 0)
            def _():
                pl.semaphore_wait(landing_free, 1)

        def ask_item(pair):
            partner_ready(pair)
            ask_back(pair).start()

        def near_item(pair):
            attend_backward(*near_attention, low, 1, 128, 8)(pair)
            partner_ready(pair)
            for which in range(2):
                hand_back(which, pair).start()

        def answer_item(pair):
            ask_back(pair).wait_recv()
            attend_backward(*far_attention, active, 1, 128, 8)(pair)
            answer_back(pair).start()

        def landed_item(pair):
            if cfg.asks:
                answer_back(pair).wait_recv()
                ask_back(pair).wait_send()
                for which in range(2):
                    hand_back(which, pair).wait_recv()
            else:
                answer_back(pair).wait_send()
                for which in range(2):
                    hand_back(which, pair).wait_send()

        def clear_item(number):
            unstage(0).wait()
            if width < 1024:
                grad_ref[...] = jnp.zeros_like(grad_ref)

        def finish_item(pair):
            at = pl.ds(pl.multiple_of(pair * tall, tall), slots)
            grad_ref[pair, :, 0:width] = (state[at, 0:width] + total[at, 0:width]).astype(
                jnp.bfloat16
            )

            @pl.when(pair == pairs - 1)
            def _():
                unstage(1).start()

        def list_backward():
            mlp_backward(1)
            norm_backward(2, 7, 5)
            backward_items(g_ref.at[7], biased(low, None))
            segments.append((pairs, self_attention_item))
            for index in range(3):
                backward_items(self_refs[index], add_total(index == 0))
            column_sums(4, 3, width)
            column_sums(6, 4, width)
            norm_backward(1, 14, 6)
            mlp_backward(0)
            norm_backward(0, 3, 2)
            backward_items(g_ref.at[3], biased(low, None))

            if cfg.asks:
                segments.append((pairs, ask_item))
                segments.append((1, clear_item))
                early = sum(count for count, _ in segments)
                segments.append((pairs, landed_item))
                backward_items(g_ref.at[0], add_total(True))
                column_sums(0, 0, 1024)
            else:
                segments.append((pairs, near_item))
                backward_items(g_ref.at[0], add_total(True))
                column_sums(0, 0, 1024)
                segments.append((1, clear_item))
                early = sum(count for count, _ in segments)
                segments.append((pairs, answer_item))
            for which in range(2):
                backward_items(own_refs[which], add_total(False))
            column_sums(2, 1, 1024)
            if not cfg.asks:
                segments.append((pairs, landed_item))
            segments.append((pairs, finish_item))
            return early, segments

        return forward, list_backward

    text_forward, text_backward = run(TEXT, text_lengths, region_counts)
    image_forward, image_backward = run(IMAGE, region_counts, text_lengths)
    pl.when(is_text)(text_forward)
    pl.when(jnp.logical_not(is_text))(image_forward)

    def run_items(step, pace, early, segments):
        spread, held, rate = pace
        every = sum(count for count, _ in segments)

        def ahead_of(turn):
            first = jnp.minimum(turn * early // spread, early)
            return jnp.minimum(first + jnp.maximum(turn - held, 0) * rate, every)

        def dispatch(item, some, start):
            if len(some) == 1:
                some[0][1](item - start)
                return
            half = len(some) // 2
            middle = start + sum(count for count, _ in some[:half])
            pl.when(item < middle)(lambda: dispatch(item, some[:half], start))
            pl.when(item >= middle)(lambda: dispatch(item, some[half:], middle))

        def one(item, carry):
            dispatch(item, segments, 0)
            return carry

        lax.fori_loop(ahead_of(step), ahead_of(step + 1), one, 0)

    def turn(step, carry):
        @pl.when(is_text)
        def _():
            run_items(step, TEXT_PACE, *text_backward())

        @pl.when(jnp.logical_not(is_text))
        def _():
            run_items(step, IMAGE_PACE, *image_backward())

        tick(step)
        return carry

    lax.fori_loop(0, unit_total + side_lag(line) + last * line_lag(line) + Z_SLOTS, turn, 0)
    unstage(1).wait()


def layer(line, text_lengths, region_counts, hidden, cotangent, weights):
    _, pairs, slots, width = hidden.shape
    tall = (slots + 15) // 16 * 16
    height = pairs * tall
    piece = 256 // line
    own_slots = slots_held(line)
    vmem = pl.BlockSpec(memory_space=pltpu.VMEM)
    smem = pl.BlockSpec(memory_space=pltpu.SMEM)
    anywhere = pl.BlockSpec(memory_space=pl.ANY)
    bf16, f32 = jnp.bfloat16, jnp.float32
    return pl.pallas_call(
        partial(layer_kernel, line, pairs, slots, tall),
        out_shape=(
            jax.ShapeDtypeStruct(hidden.shape, bf16),
            jax.ShapeDtypeStruct(hidden.shape, bf16),
            jax.ShapeDtypeStruct((piece, OUT_BLOCKS * UNIT), f32),
        ),
        in_specs=[smem] * 2 + [anywhere] * 8 + [vmem] * 5,
        out_specs=(anywhere,) * 3,
        scratch_shapes=[
            pltpu.VMEM((12, 2, 2, 256, height), bf16),
            pltpu.VMEM((16, height, 1024), bf16),
            pltpu.VMEM((32, 1024), f32),
            pltpu.VMEM((8, 3072), f32),
            pltpu.VMEM((2,) + hidden.shape[1:], bf16),
            pltpu.VMEM((RING, 1024, 1024), bf16),
            pltpu.VMEM((pairs * 2 * SHORT, 1024), bf16),
            pltpu.VMEM((height, 1024), bf16),
            pltpu.VMEM((height, 1024), f32),
            pltpu.VMEM((height, 1024), f32),
            pltpu.VMEM((height, 1024), bf16),
            pltpu.VMEM((height, 1024), bf16),
            pltpu.VMEM((3, height, 1024), bf16),
            pltpu.VMEM((height, 4), f32),
            pltpu.VMEM((pairs, 8, 128, tall), bf16),
            pltpu.VMEM((pairs, 16, 112, tall), bf16),
            pltpu.VMEM((16, 1024), f32),
            pltpu.VMEM((8, 3072), f32),
            pltpu.SemaphoreType.DMA((RING,)),
            pltpu.SemaphoreType.DMA((3, pairs)),
            pltpu.SemaphoreType.DMA((3, pairs)),
            pltpu.SemaphoreType.DMA((3, pairs)),
            pltpu.SemaphoreType.DMA((3, pairs)),
            pltpu.SemaphoreType.REGULAR,
            pltpu.SemaphoreType.DMA((2,)),
            pltpu.VMEM((CORE_SLOTS, 2, 256, UNIT), bf16),
            pltpu.VMEM((CORE_SLOTS, 2, 256, UNIT), bf16),
            pltpu.VMEM((2, 2, 256, UNIT), f32),
            pltpu.VMEM((2 * side_lag(line), 256, UNIT), bf16),
            pltpu.VMEM((2 * side_lag(line), 256, UNIT), bf16),
            pltpu.VMEM((own_slots, 256, UNIT), f32),
            pltpu.VMEM((Z_SLOTS, 256, UNIT), bf16),
            pltpu.VMEM((Z_SLOTS, 256, UNIT), bf16),
            pltpu.VMEM((Z_SLOTS, 256, UNIT), bf16),
            pltpu.VMEM((Z_SLOTS, 256, UNIT), bf16),
            pltpu.SemaphoreType.DMA((2, CORE_SLOTS)),
            pltpu.SemaphoreType.DMA((2, 2 * side_lag(line))),
            pltpu.SemaphoreType.DMA((2, Z_SLOTS, line)),
            pltpu.SemaphoreType.DMA((2, Z_SLOTS, line)),
            pltpu.SemaphoreType.REGULAR,
            pltpu.SemaphoreType.REGULAR,
            pltpu.SemaphoreType.DMA((SUM_SLOTS,)),
            pltpu.SemaphoreType.DMA((-(-OUT_BLOCKS * UNIT // 1024),)),
        ],
        compiler_params=pltpu.CompilerParams(
            collective_id=0, has_side_effects=True, vmem_limit_bytes=VMEM_BYTES
        ),
        name="layer",
    )(text_lengths, region_counts, hidden, cotangent, *weights)


def place_kernel(
    line,
    result_in,
    grad_in,
    sums,
    result,
    grad,
    co_qkv,
    co_out,
    self_qkv,
    self_out,
    mlp_up,
    mlp_down,
    proj_bias,
    bias_up,
    bias_down,
    gain,
    shift,
    sems,
):
    piece = 256 // line

    def taken(first, width):
        return sums.at[:, pl.ds(first * UNIT, width)]

    moves = [
        (result_in, result),
        (grad_in, grad),
        (taken(12, 1024), co_out.at[0]),
        (taken(28, 1024), self_out.at[0]),
        (taken(32, 3072), mlp_up.at[0, 0]),
        (taken(44, 3072), mlp_up.at[0, 1]),
    ]
    for index in range(3):
        rows = pl.ds(index * piece, piece)
        moves += [
            (taken(4 * index, 1024), co_qkv.at[0, index]),
            (taken(16 + 4 * index, 1024), self_qkv.at[0, index]),
            (taken(56 + 4 * index, 1024), mlp_down.at[0, 0, rows]),
            (taken(68 + 4 * index, 1024), mlp_down.at[0, 1, rows]),
        ]
    copies = [
        pltpu.make_async_copy(source, target, sems.at[index])
        for index, (source, target) in enumerate(moves)
    ]
    for copy in copies:
        copy.start()
    rows = sums[:, 80 * UNIT : 80 * UNIT + LANES].T
    for half in range(2):
        proj_bias[0, half] = rows[3 * half : 3 * half + 3]
        for group in range(3):
            bias_up[0, half : half + 1, group * piece : (group + 1) * piece] = rows[
                6 + 3 * half + group : 7 + 3 * half + group
            ]
    bias_down[0] = rows[12:14]
    gain[0] = rows[14:18]
    shift[0] = rows[18:22]
    for copy in copies:
        copy.wait()


def place(line, result, grad, sums):
    piece = sums.shape[0]
    vmem = pl.BlockSpec(memory_space=pltpu.VMEM)
    anywhere = pl.BlockSpec(memory_space=pl.ANY)
    shapes = (
        (1, 3, piece, 1024),
        (1, piece, 1024),
        (1, 3, piece, 1024),
        (1, piece, 1024),
        (1, 2, piece, 3072),
        (1, 2, 3 * piece, 1024),
        (1, 2, 3, piece),
        (1, 2, 3 * piece),
        (1, 2, piece),
        (1, 4, piece),
        (1, 4, piece),
    )
    return pl.pallas_call(
        partial(place_kernel, line),
        out_shape=tuple(jax.ShapeDtypeStruct(result.shape, result.dtype) for _ in range(2))
        + tuple(jax.ShapeDtypeStruct(shape, jnp.float32) for shape in shapes),
        in_specs=[vmem] * 3,
        out_specs=(anywhere,) * 8 + (vmem,) * 5,
        scratch_shapes=[
            pltpu.SemaphoreType.DMA((18,)),
        ],
        name="place",
    )(result, grad, sums)


def on_device(
    hidden,
    text_lengths,
    region_counts,
    co_qkv,
    co_out,
    self_qkv,
    self_out,
    mlp_up,
    mlp_down,
    proj_bias,
    mlp_bias_up,
    mlp_bias_down,
    norm_gain_table,
    norm_bias,
    cotangent,
):
    line = lax.axis_size("dp") // 4
    result, grad, sums = layer(
        line,
        text_lengths,
        region_counts,
        hidden,
        cotangent,
        (
            co_qkv,
            co_out,
            self_qkv,
            self_out,
            mlp_up,
            mlp_down,
            proj_bias,
            mlp_bias_up,
            mlp_bias_down,
            norm_gain_table,
            norm_bias,
        ),
    )
    return place(line, result, grad, sums)


def solution(mesh):
    return jax.shard_map(
        on_device,
        mesh=mesh,
        in_specs=(
            P("stream", "dp", None, None),
            P("dp"),
            P("dp"),
            P("stream", None, None, None),
            P("stream", None, None),
            P("stream", None, None, None),
            P("stream", None, None),
            P("stream", None, None, None),
            P("stream", None, None, None),
            P("stream", None, None, None),
            P("stream", None, None),
            P("stream", None, None),
            P("stream", None, None),
            P("stream", None, None),
            P("stream", "dp", None, None),
        ),
        out_specs=(
            P("stream", "dp", None, None),
            P("stream", "dp", None, None),
            P("stream", None, "dp", None),
            P("stream", "dp", None),
            P("stream", None, "dp", None),
            P("stream", "dp", None),
            P("stream", None, "dp", None),
            P("stream", None, "dp", None),
            P("stream", None, None, "dp"),
            P("stream", None, "dp"),
            P("stream", None, "dp"),
            P("stream", None, "dp"),
            P("stream", None, "dp"),
        ),
        check_vma=False,
    )
```

profile of v0, /device:TPU:0, one launch (start us, length us, event | category | flops | bytes accessed | tf_op | source)
XLA Modules:
  0.0 312.5 jit_solution(8466548608373808567)
XLA Ops:
  0.6 1.3 copy.30.proj_bias
  2.0 2.3 copy.28.hidden
  4.3 2.3 copy.29.cotangent
  6.6 292.5 %layer.1 = (bf16[1,4,100,1024]{3,2,1,0:T(8,128)(2,1)}, bf16[1,4,100,1024]{3,2,1,0:T(8,128)(2,1)}, f32[64,20736]{1,0:T(8,128)}) custom-call(s32[4]{0:T(128)} %text_lengths.1, s32[4]{0:T(128)} %region_counts.1, bf16[1,4,100,1024]{3,2,1,0:T(8,128)(2,1)} %copy.28.hidden, bf16[1,4,100,1024]{3,2,1,0:T(8,128)(2,1)} %copy.29.cotangent, ...), custom_call_target="tpu_custom_call" | custom-call | tf_op jit(solution)/shard_map/layer/pallas_call | solution.py:1246
  299.1 6.6 %place.1 = (bf16[1,4,100,1024]{3,2,1,0:T(8,128)(2,1)}, bf16[1,4,100,1024]{3,2,1,0:T(8,128)(2,1)}, f32[1,3,64,1024]{3,2,1,0:T(8,128)}, f32[1,64,1024]{2,1,0:T(8,1...) custom-call(bf16[1,4,100,1024]{3,2,1,0:T(8,128)(2,1)} %get-tuple-ele, ...), custom_call_target="tpu_custom_call" | custom-call | tf_op jit(solution)/shard_map/place/pallas_call | solution.py:1385
  305.7 2.7 copy.31
  308.4 1.3 copy.33
  309.6 2.7 copy.32
where the time goes:
time: 315 us; the launch traced here: 313 us
  Pallas kernels  299 us (95%)
  local copies, waits for them, and re-layouts  12.5 us (4%)
    pallas_call x1, Pallas kernels, layer(): pl.pallas_call(partial(layer_kernel, line, pairs, slots, tall), out_shape...  292 us
    pallas_call x1, Pallas kernels, place(): pl.pallas_call(partial(place_kernel, line), out_shape=tuple((jax.ShapeDty...  6.64 us
    pallas_call x3, local copies, waits for them, and re-layouts, place(): pl.pallas_call(partial(place_kernel, line), out_shape=tuple((jax.ShapeDty...  6.62 us

commit v1 on v0

--- a/solution.py
+++ b/solution.py
@@ -242,16 +242,13 @@
             mlp_down_whole,
         )
     )
-    hidden_ref, cotangent_ref = staged.at[0], staged.at[1]
-    result_ref, grad_ref = staged.at[0], staged.at[1]
 
     def stage(index):
         source = (hidden, cotangent)[index]
         return pltpu.make_async_copy(source.at[0], staged.at[index], staged_sems.at[index])
 
     def unstage(index):
-        target = (result, grad)[index]
-        return pltpu.make_async_copy(staged.at[index], target.at[0], staged_sems.at[index])
+        return pltpu.make_async_copy(low, (result, grad)[index], staged_sems.at[index])
 
     stage(0).start()
     stage(1).start()
@@ -273,8 +270,10 @@
     pl.semaphore_wait(
         barrier, 3 + (spot > 0).astype(jnp.int32) + (spot < last).astype(jnp.int32)
     )
-    for half in range(2):
-        params[3 * half : 3 * half + 3] = proj_bias[0, half].astype(jnp.float32)
+    for index in range(3):
+        for half in range(2):
+            row = 3 * half + index
+            params[row : row + 1] = proj_bias[0, index, half : half + 1].astype(jnp.float32)
     params[6:8] = bias_down[0].astype(jnp.float32)
     params[8:12] = gain[0].astype(jnp.float32)
     params[12:16] = shift[0].astype(jnp.float32)
@@ -910,7 +909,7 @@
 
             def body(pair):
                 length = lengths[pair]
-                for group in range(group_count):
+                def one_group(group):
                     at = pl.ds(group * LANES, LANES)
                     key = stacked(keys[key_rows(pair), at], split)
                     value = stacked(values[key_rows(pair), at], split)
@@ -940,13 +939,16 @@
                         preferred_element_type=jnp.float32,
                     ).astype(jnp.bfloat16)
 
+                for group in range(group_count):
+                    one_group(group)
+
             return body
 
         def attend_backward(query, keys, values, key_rows, probs, source, split, head, group_count):
             scale = 1.0 / math.sqrt(head)
 
             def body(pair):
-                for group in range(group_count):
+                def one_group(group):
                     at = pl.ds(group * LANES, LANES)
                     key = stacked(keys[key_rows(pair), at], split)
                     value = stacked(values[key_rows(pair), at], split)
@@ -981,6 +983,9 @@
                     keys[key_rows(pair), at] = grad_key.astype(jnp.bfloat16)
                     values[key_rows(pair), at] = grad_value.astype(jnp.bfloat16)
 
+                for group in range(group_count):
+                    one_group(group)
+
             return body
 
         def clear_tail(ref, pair, count):
@@ -1014,7 +1019,7 @@
             low[...] = jnp.zeros_like(low)
             stage(0).wait()
             for pair in range(pairs):
-                low[pair * tall : pair * tall + slots, 0:width] = hidden_ref[pair, :, 0:width]
+                low[pair * tall : pair * tall + slots, 0:width] = staged[0, :, pair, 0:width]
             for index in cfg.order:
                 forward_product(low, biased(g_ref.at[index], (0, None, 1)[index]))
                 if cfg.asks and index == 0:
@@ -1074,31 +1079,28 @@
             forward_product(low, add_total(True))
             norm_forward(2, 5, 5)
             mlp_forward(1)
-            if not cfg.asks:
-                for pair in range(pairs):
-                    clear_rest(active, pair)
-                pl.semaphore_signal(landing_free, inc=1, device_id=partner, device_id_type=MESH)
-
-            if width < 1024:
-                result_ref[...] = jnp.zeros_like(result_ref)
+
             stage(1).wait()
+            for pair in range(pairs):
+                active[pair * tall : pair * tall + slots] = staged[1, :, pair]
+                active[pair * tall + slots : (pair + 1) * tall] = jnp.zeros(
+                    (tall - slots, 1024), jnp.bfloat16
+                )
 
             def last_norm(pair):
                 at = pair_rows(pair)
                 rows, inverse = normalize(
                     state[at, 0:width] + total[at, 0:width] + params[7:8, 0:width]
                 )
-                result = rows * params[11:12, 0:width] + params[15:16, 0:width]
-                result_ref[pair, :, 0:width] = result[0:slots].astype(jnp.bfloat16)
-                total[at, 0:width] = jnp.zeros((tall, width), jnp.float32)
-                total[pl.ds(pl.multiple_of(pair * tall, tall), slots), 0:width] = cotangent_ref[
-                    pair, :, 0:width
-                ].astype(jnp.float32)
-                norm_gradient(3, at, total[at, 0:width], rows, inverse, 15, 7)
+                output = rows * params[11:12, 0:width] + params[15:16, 0:width]
+                low[at, 0:width] = output.astype(jnp.bfloat16)
+                gradient = active[at, 0:width].astype(jnp.float32)
+                norm_gradient(3, at, gradient, rows, inverse, 15, 7)
 
             for_pairs(last_norm)
             unstage(0).start()
-
+            if not cfg.asks:
+                pl.semaphore_signal(landing_free, inc=1, device_id=partner, device_id_type=MESH)
 
         def self_attention_item(pair):
             attend_backward(*self_attention, low, cfg.split, cfg.head, groups)(pair)
@@ -1136,16 +1138,14 @@
                 for which in range(2):
                     hand_back(which, pair).wait_send()
 
-        def clear_item(number):
+        def shown_item(number):
             unstage(0).wait()
+
+        def finish_item(pair):
+            at = pair_rows(pair)
+            low[at, 0:width] = (state[at, 0:width] + total[at, 0:width]).astype(jnp.bfloat16)
             if width < 1024:
-                grad_ref[...] = jnp.zeros_like(grad_ref)
-
-        def finish_item(pair):
-            at = pl.ds(pl.multiple_of(pair * tall, tall), slots)
-            grad_ref[pair, :, 0:width] = (state[at, 0:width] + total[at, 0:width]).astype(
-                jnp.bfloat16
-            )
+                low[at, width:1024] = jnp.zeros((tall, 1024 - width), jnp.bfloat16)
 
             @pl.when(pair == pairs - 1)
             def _():
@@ -1154,6 +1154,7 @@
         def list_backward():
             mlp_backward(1)
             norm_backward(2, 7, 5)
+            segments.append((1, shown_item))
             backward_items(g_ref.at[7], biased(low, None))
             segments.append((pairs, self_attention_item))
             for index in range(3):
@@ -1167,7 +1168,6 @@
 
             if cfg.asks:
                 segments.append((pairs, ask_item))
-                segments.append((1, clear_item))
                 early = sum(count for count, _ in segments)
                 segments.append((pairs, landed_item))
                 backward_items(g_ref.at[0], add_total(True))
@@ -1176,7 +1176,6 @@
                 segments.append((pairs, near_item))
                 backward_items(g_ref.at[0], add_total(True))
                 column_sums(0, 0, 1024)
-                segments.append((1, clear_item))
                 early = sum(count for count, _ in segments)
                 segments.append((pairs, answer_item))
             for which in range(2):
@@ -1234,7 +1233,7 @@
 
 
 def layer(line, text_lengths, region_counts, hidden, cotangent, weights):
-    _, pairs, slots, width = hidden.shape
+    _, slots, pairs, width = hidden.shape
     tall = (slots + 15) // 16 * 16
     height = pairs * tall
     piece = 256 // line
@@ -1246,8 +1245,8 @@
     return pl.pallas_call(
         partial(layer_kernel, line, pairs, slots, tall),
         out_shape=(
-            jax.ShapeDtypeStruct(hidden.shape, bf16),
-            jax.ShapeDtypeStruct(hidden.shape, bf16),
+            jax.ShapeDtypeStruct((height, width), bf16),
+            jax.ShapeDtypeStruct((height, width), bf16),
             jax.ShapeDtypeStruct((piece, OUT_BLOCKS * UNIT), f32),
         ),
         in_specs=[smem] * 2 + [anywhere] * 8 + [vmem] * 5,
@@ -1308,7 +1307,7 @@
     line,
     result_in,
     grad_in,
-    sums,
+    sums_in,
     result,
     grad,
     co_qkv,
@@ -1322,38 +1321,59 @@
     bias_down,
     gain,
     shift,
+    sums,
+    rows_in,
+    in_sems,
     sems,
 ):
     piece = 256 // line
-
-    def taken(first, width):
-        return sums.at[:, pl.ds(first * UNIT, width)]
+    _, slots, pairs, _ = result.shape
+    tall = result_in.shape[0] // pairs
+
+    def span(first, width):
+        return pl.ds(first * UNIT, width)
 
     moves = [
-        (result_in, result),
-        (grad_in, grad),
-        (taken(12, 1024), co_out.at[0]),
-        (taken(28, 1024), self_out.at[0]),
-        (taken(32, 3072), mlp_up.at[0, 0]),
-        (taken(44, 3072), mlp_up.at[0, 1]),
+        (span(80, UNIT), None),
+        (span(12, 1024), co_out.at[0]),
+        (span(28, 1024), self_out.at[0]),
+        (span(32, 3072), mlp_up.at[0, 0]),
+        (span(44, 3072), mlp_up.at[0, 1]),
     ]
     for index in range(3):
         rows = pl.ds(index * piece, piece)
         moves += [
-            (taken(4 * index, 1024), co_qkv.at[0, index]),
-            (taken(16 + 4 * index, 1024), self_qkv.at[0, index]),
-            (taken(56 + 4 * index, 1024), mlp_down.at[0, 0, rows]),
-            (taken(68 + 4 * index, 1024), mlp_down.at[0, 1, rows]),
+            (span(4 * index, 1024), co_qkv.at[0, index]),
+            (span(16 + 4 * index, 1024), self_qkv.at[0, index]),
+            (span(56 + 4 * index, 1024), mlp_down.at[0, 0, rows]),
+            (span(68 + 4 * index, 1024), mlp_down.at[0, 1, rows]),
         ]
-    copies = [
-        pltpu.make_async_copy(source, target, sems.at[index])
-        for index, (source, target) in enumerate(moves)
+    whole = [
+        pltpu.make_async_copy(source, rows_in.at[index], sems.at[index])
+        for index, source in enumerate((result_in, grad_in))
     ]
-    for copy in copies:
+    loads = [
+        pltpu.make_async_copy(sums_in.at[:, at], sums.at[:, at], in_sems.at[index])
+        for index, (at, _) in enumerate(moves)
+    ]
+    stores = [
+        pltpu.make_async_copy(sums.at[:, at], target, sems.at[2 + index])
+        for index, (at, target) in enumerate(moves[1:])
+    ]
+    for copy in whole + loads:
         copy.start()
+    for index, target in enumerate((result, grad)):
+        whole[index].wait()
+        for pair in range(pairs):
+            target[0, :, pair, :] = rows_in[index, pair * tall : pair * tall + slots]
+    loads[0].wait()
+    for load, store in zip(loads[1:], stores, strict=True):
+        load.wait()
+        store.start()
     rows = sums[:, 80 * UNIT : 80 * UNIT + LANES].T
     for half in range(2):
-        proj_bias[0, half] = rows[3 * half : 3 * half + 3]
+        for index in range(3):
+            proj_bias[0, index, half : half + 1] = rows[3 * half + index : 3 * half + index + 1]
         for group in range(3):
             bias_up[0, half : half + 1, group * piece : (group + 1) * piece] = rows[
                 6 + 3 * half + group : 7 + 3 * half + group
@@ -1361,11 +1381,11 @@
     bias_down[0] = rows[12:14]
     gain[0] = rows[14:18]
     shift[0] = rows[18:22]
-    for copy in copies:
-        copy.wait()
-
-
-def place(line, result, grad, sums):
+    for store in stores:
+        store.wait()
+
+
+def place(line, slots, pairs, result, grad, sums):
     piece = sums.shape[0]
     vmem = pl.BlockSpec(memory_space=pltpu.VMEM)
     anywhere = pl.BlockSpec(memory_space=pl.ANY)
@@ -1376,21 +1396,26 @@
         (1, piece, 1024),
         (1, 2, piece, 3072),
         (1, 2, 3 * piece, 1024),
-        (1, 2, 3, piece),
+        (1, 3, 2, piece),
         (1, 2, 3 * piece),
         (1, 2, piece),
         (1, 4, piece),
         (1, 4, piece),
     )
+    rows = jax.ShapeDtypeStruct((1, slots, pairs, 1024), result.dtype)
     return pl.pallas_call(
         partial(place_kernel, line),
-        out_shape=tuple(jax.ShapeDtypeStruct(result.shape, result.dtype) for _ in range(2))
+        out_shape=(rows, rows)
         + tuple(jax.ShapeDtypeStruct(shape, jnp.float32) for shape in shapes),
-        in_specs=[vmem] * 3,
-        out_specs=(anywhere,) * 8 + (vmem,) * 5,
+        in_specs=[anywhere] * 3,
+        out_specs=(vmem,) * 2 + (anywhere,) * 6 + (vmem,) * 5,
         scratch_shapes=[
+            pltpu.VMEM(sums.shape, jnp.float32),
+            pltpu.VMEM((2,) + result.shape, result.dtype),
+            pltpu.SemaphoreType.DMA((17,)),
             pltpu.SemaphoreType.DMA((18,)),
         ],
+        compiler_params=pltpu.CompilerParams(vmem_limit_bytes=62 * 1024 * 1024),
         name="place",
     )(result, grad, sums)
 
@@ -1417,8 +1442,8 @@
         line,
         text_lengths,
         region_counts,
-        hidden,
-        cotangent,
+        jnp.swapaxes(hidden, 1, 2),
+        jnp.swapaxes(cotangent, 1, 2),
         (
             co_qkv,
             co_out,
@@ -1426,14 +1451,18 @@
             self_out,
             mlp_up,
             mlp_down,
-            proj_bias,
+            jnp.swapaxes(proj_bias, 1, 2),
             mlp_bias_up,
             mlp_bias_down,
             norm_gain_table,
             norm_bias,
         ),
     )
-    return place(line, result, grad, sums)
+    outputs = place(line, hidden.shape[2], hidden.shape[1], result, grad, sums)
+    return tuple(
+        jnp.swapaxes(output, 1, 2) if index in (0, 1, 8) else output
+        for index, output in enumerate(outputs)
+    )
 
 
 def solution(mesh):

time: 315 us -> 306 us (0.971)
  local copies, waits for them, and re-layouts: 12.5 us -> 0 us
    pallas_call x3 -> x0, local copies, waits for them, and re-layouts: 6.62 us -> none  [place(): pl.pallas_call(partial(place_kernel, line), out_shape=tuple((jax.ShapeDty...]
    unnamed x3 -> x0, local copies, waits for them, and re-layouts: 5.91 us -> none
where the time goes in v1:
time: 306 us; the launch traced here: 302 us
  Pallas kernels  302 us (99%)
    pallas_call x1, Pallas kernels, layer(): pl.pallas_call(partial(layer_kernel, line, pairs, slots, tall), out_shape...  294 us
    pallas_call x1, Pallas kernels, place(): pl.pallas_call(partial(place_kernel, line), out_shape=(rows, rows) + tupl...  7.51 us

profile of v1, /device:TPU:0, one launch (start us, length us, event | category | flops | bytes accessed | tf_op | source)
XLA Modules:
  0.0 302.4 jit_solution(13267161135665700118)
XLA Ops:
  0.7 294.0 %layer.1 = (bf16[448,1024]{1,0:T(8,128)(2,1)}, bf16[448,1024]{1,0:T(8,128)(2,1)}, f32[64,20736]{1,0:T(8,128)}) custom-call(s32[4]{0:T(128)} %text_lengths.1, s32[4]{0:T(128)} %region_counts.1, bf16[1,100,4,1024]{3,2,1,0:T(4,128)(2,1)} %bitcast.6, bf16[1,100,4,1024]{3,2,1,0:T(4,128)(2,1)} %bitcast.7, bf16[1,3,1024,1024]{3,2,1,0:T(8,128)(2,1)} %co_qkv_whole.1, ...), custom_call_target="tpu_custom_call" | custom-call | tf_op jit(solution)/shard_map/layer/pallas_call | solution.py:1245
  294.7 7.5 %place.1 = (bf16[1,100,4,1024]{3,2,1,0:T(4,128)(2,1)}, bf16[1,100,4,1024]{3,2,1,0:T(4,128)(2,1)}, f32[1,3,64,1024]{3,2,1,0:T(8,128)}, f32[1,64,1024]{2,1,0:T(8,1...) custom-call(bf16[448,1024]{1,0:T(8,128)(2,1)} %get-tuple-element.29., ...), custom_call_target="tpu_custom_call" | custom-call | tf_op jit(solution)/shard_map/place/pallas_call | solution.py:1406
